TPU v7x, 256 devices: a whole 4x4x8 slice. The times are simulated.
256 devices in a mesh: rows: 64 (over z, x, core), cols: 4 (over y).
Axes of the slice: x: 4, y: 4, z: 8, core: 2. Of those that a mesh axis runs over, the one named last changes fastest.
Arguments:
- embeddings: bfloat16 [65536, 512], P('rows'), may hold values from -90 to 90
- neighbours: int32 [256, 12], P('rows'), may hold values from -1 to 255, as said below
- queries: float32 [65536, 512], P('rows', 'cols'), may hold values from -22 to 22
Outputs:
- diffused: float32 [65536, 512], P('rows', 'cols')
Inputs may be any that keep to these rules, and one draw needn't show every extreme that they name: `neighbours`: row b lists in rising order the distinct blocks linked to block b, then -1 in the remaining slots. Every block is linked to itself, links are symmetric, and a linked block lies on the same index of rows as b or on an adjacent one, block c lying on index c // 4. Some block has 12 links.
All inputs are finite; a program needn't handle non-finite values.
Results may differ from a plain program's by a relative error of at most 0.00039.
Values may be sent and summed in bfloat16 or wider, within the bound.
No kernel may reach another device: no remote copies, remote signals or barrier semaphores. Data moves between devices by JAX's collectives and lax.ppermute only.
A program may use at most 128 MiB of HBM per device.

v0:
```python
import jax
import jax.numpy as jnp
from jax import lax
from jax.sharding import PartitionSpec as P

ITERS = 3
diffusion = 0.9
epsilon = 1e-06
highest = lax.Precision.HIGHEST
contract_rows = (((1,), (1,)), ((), ()))


def extended(array, sides, width):
    for axis, dim in sides:
        peers, length = (lax.axis_size(axis), array.shape[dim])
        up = [(i, (i + 1) % peers) for i in range(peers - 1)]
        down = [(j, i) for i, j in up]
        last = lax.slice_in_dim(array, length - width, length, axis=dim)
        leading = lax.slice_in_dim(array, 0, width, axis=dim)
        before = lax.ppermute(last, axis, up)
        after = lax.ppermute(leading, axis, down)
        array = jnp.concatenate([before, array, after], axis=dim)
    return array


def column_sums(left_side, right_side):
    return jnp.sum(left_side * right_side, axis=0)


def squares(residual):
    return lax.psum(column_sums(residual, residual), "rows")


def shards(embeddings, neighbours, queries):
    own_blocks = neighbours.shape[0]
    own_rows = embeddings.shape[0]
    block_rows = own_rows // own_blocks
    features = embeddings.shape[1]
    values = embeddings.astype(jnp.float32)
    normed = (values * lax.rsqrt(jnp.sum(values * values, axis=1, keepdims=True) + epsilon)).astype(
        jnp.bfloat16
    )
    stacked = normed.reshape(own_blocks, block_rows, features)
    beside_all = extended(stacked, (("rows", 0),), own_blocks)
    similar = lax.dot_general(
        normed,
        beside_all.reshape(3 * own_rows, features),
        contract_rows,
        preferred_element_type=jnp.float32,
    )
    lowest = (lax.axis_index("rows") - 1) * own_blocks
    candidates = lowest + jnp.arange(3 * own_blocks, dtype=jnp.int32)
    linked = jnp.any(neighbours[:, :, None] == candidates[None, None, :], axis=1).astype(
        jnp.float32
    )
    cubed = jnp.maximum(similar, 0.0) ** 3
    affinity = (
        cubed.reshape(own_blocks, block_rows, 3 * own_blocks, block_rows) * linked[:, None, :, None]
    ).reshape(own_rows, 3 * own_rows)
    inv_root = lax.rsqrt(jnp.sum(affinity, axis=1))
    far_roots = extended(inv_root.reshape(own_blocks, block_rows), (("rows", 0),), own_blocks)
    banded = affinity * inv_root[:, None] * far_roots.reshape(1, 3 * own_rows)
    solution = jnp.zeros_like(queries)
    residual = queries
    direction = queries
    residual_sq = squares(residual)
    for iteration in range(ITERS):
        columns = direction.shape[1]
        outgoing = direction
        nearby = extended(
            outgoing.reshape(own_blocks, block_rows, columns), (("rows", 0),), own_blocks
        )
        mixed = jnp.dot(
            banded,
            nearby.reshape(3 * own_rows, columns),
            precision=highest,
            preferred_element_type=jnp.float32,
        )
        image = direction - diffusion * mixed
        curvature = lax.psum(column_sums(direction, image), "rows")
        step_size = residual_sq / curvature
        solution = solution + step_size * direction
        residual = residual - step_size * image
        if iteration + 1 < ITERS:
            updated = squares(residual)
            direction = residual + updated / residual_sq * direction
            residual_sq = updated
    return solution


def solution(mesh):
    placed = (P("rows", None), P("rows", None), P("rows", "cols"))
    return jax.shard_map(
        shards, mesh=mesh, in_specs=placed, out_specs=P("rows", "cols"), check_vma=False
    )
```

profile of v0, /device:TPU:145, one launch (start us, length us, event | category | flops | bytes accessed | tf_op | source)
XLA Modules:
  0.0 768.8 jit_solution(9624634156711667488)
XLA Ops:
  0.0 1.6 fusion.10
  1.6 1.5 fusion.11
  3.1 2.6 collective-permute-start.1
  5.7 3.0 collective-permute-start
  8.7 0.0 copy-done
  8.7 2.6 collective-permute-start.5
  11.3 3.0 collective-permute-start.4
  14.3 0.0 copy-done.1
  14.3 0.1 copy.5
  14.4 0.1 compare_reduce_fusion
  14.5 0.1 copy.6
  14.6 6.2 mul.127
  20.8 12.3 %copy.8 = f32[384,8,4,256]{3,1,2,0:T(8,128)} copy(f32[384,8,4,256]{3,2,1,0:T(4,128)} %bitcast.18) | data formatting | bytes 25165824
  33.1 12.6 %copy.7 = f32[1024,3072]{1,0:T(8,128)} copy(f32[1024,3072]{0,1:T(8,128)} %bitcast.19) | data formatting | bytes 25165824 | tf_op jit(solution)/shard_map/mul | solution.py:58
  45.7 0.0 collective-permute-done.1
  45.7 0.0 collective-permute-done
  45.7 1.4 pad_maximum_fusion
  47.1 9.5 %fusion.20 = (f32[1024]{0:T(1024)S(1)}, f32[1024,3072]{1,0:T(8,128)}) fusion(f32[1024,3072]{1,0:T(8,128)} %copy.7, bf16[1024,512]{1,0:T(8,128)(2,1)S(1)} %fusion.11, bf16[3072,512]{1,0:T(8,128)(2,1)S(1)} %bitcast.29), kind=kOutput, calls=%fused_computation.42 | convolution fusion | flops 3236953088 | bytes 29364224 | tf_op jit(solution)/shard_map/dot_general | solution.py:45
  56.6 5.9 collective-permute-start.3
  62.5 2.1 collective-permute-start.2
  64.6 0.0 collective-permute-done.5
  64.6 0.0 collective-permute-done.4
  64.6 1.1 pad_maximum_fusion.1
  65.8 0.0 collective-permute-done.3
  65.8 4.3 collective-permute-done.2
  70.2 13.3 %multiply_reduce_fusion.3 = (f32[128]{0:T(128)S(1)}, f32[128]{0:T(128)S(1)}, f32[1024,128]{1,0:T(8,128)S(1)}) fusion(f32[1024,128]{1,0:T(8,128)S(1)} %copy-done, f32[3072,128]{1,0:T(8,128)S(1)} %bitcast.33, f32[1024,3072]{1,0:T(8,128)} %get-tuple-element.12, f32[3072]{0:T(1024)S(1)} %mul.132, f32[1024]{0:T(1024)S(1)} %rsqrt.20), kind=kOutput, calls=%fused_computation.36 | convolution fusion | flops 4838916096 | bytes 15221760 | tf_op jit(solution)/shard_map/dot_general | solution.py:73
  83.5 129.1 %all-reduce = (f32[128]{0:T(128)S(1)}, f32[128]{0:T(128)S(1)}) all-reduce(f32[128]{0:T(128)S(1)} %get-tuple-element.6, f32[128]{0:T(128)S(1)} %get-tuple-element.5), channel_id=1, replica_groups=mesh['rows'=64,'cols'=4] {'rows'}, use_global_device_ids=true, to_apply=%region_1.0 | all-reduce | flops 256 | bytes 2048 | tf_op jit(solution)/shard_map/psum | solution.py:31
  212.6 0.2 multiply_reduce_fusion.2
  212.7 124.1 %psum.44 = f32[128]{0:T(128)S(1)} all-reduce(f32[128]{0:T(128)S(1)} %get-tuple-element.9), channel_id=1, replica_groups=mesh['rows'=64,'cols'=4] {'rows'}, use_global_device_ids=true, to_apply=%region_8.0 | all-reduce | flops 128 | bytes 1024 | tf_op jit(solution)/shard_map/psum | solution.py:31
  336.9 0.1 multiply_add_fusion.2
  336.9 2.6 collective-permute-start.7
  339.5 3.0 collective-permute-start.6
  342.5 5.2 collective-permute-done.7
  347.7 0.9 collective-permute-done.6
  348.6 0.1 pad_maximum_fusion.2
  348.7 13.3 %multiply_reduce_fusion.1 = (f32[128]{0:T(128)S(1)}, f32[1024,128]{1,0:T(8,128)S(1)}) fusion(f32[1024,128]{1,0:T(8,128)S(1)} %multiply_add_fusion.2, f32[3072,128]{1,0:T(8,128)S(1)} %bitcast.35, f32[1024,3072]{1,0:T(8,128)} %get-tuple-element.12, f32[3072]{0:T(1024)S(1)} %mul.132, f32[1024]{0:T(1024)S(1)} %rsqrt.20), kind=kOutput, calls=%fused_computation.32 | convolution fusion | flops 4838653952 | bytes 15221248 | tf_op jit(solution)/shard_map/dot_general | solution.py:73
  362.1 128.3 %psum.45 = f32[128]{0:T(128)S(1)} all-reduce(f32[128]{0:T(128)S(1)} %get-tuple-element.14), channel_id=1, replica_groups=mesh['rows'=64,'cols'=4] {'rows'}, use_global_device_ids=true, to_apply=%region_10.0 | all-reduce | flops 128 | bytes 1024 | tf_op jit(solution)/shard_map/psum | solution.py:80
  490.4 0.2 multiply_reduce_fusion
  490.6 124.1 %psum.46 = f32[128]{0:T(128)S(1)} all-reduce(f32[128]{0:T(128)S(1)} %multiply_reduce_fusion), channel_id=1, replica_groups=mesh['rows'=64,'cols'=4] {'rows'}, use_global_device_ids=true, to_apply=%region_12.0 | all-reduce | flops 128 | bytes 1024 | tf_op jit(solution)/shard_map/psum | solution.py:31
  614.7 0.1 multiply_add_fusion.1
  614.7 2.6 collective-permute-start.9
  617.3 3.0 collective-permute-start.8
  620.3 5.2 collective-permute-done.9
  625.5 0.9 collective-permute-done.8
  626.4 0.1 pad_maximum_fusion.3
  626.5 13.2 %fusion.19 = f32[128]{0:T(128)S(1)} fusion(f32[1024,128]{1,0:T(8,128)S(1)} %multiply_add_fusion.1, f32[3072,128]{1,0:T(8,128)S(1)} %bitcast.34, f32[1024,3072]{1,0:T(8,128)} %get-tuple-element.12, f32[3072]{0:T(1024)S(1)} %mul.132, f32[1024]{0:T(1024)S(1)} %rsqrt.20), kind=kOutput, calls=%fused_computation.27 | convolution fusion | flops 4838653952 | bytes 14696960 | tf_op jit(solution)/shard_map/dot_general | solution.py:73
  639.8 128.1 %psum.47 = f32[128]{0:T(128)S(1)} all-reduce(f32[128]{0:T(128)S(1)} %fusion.19), channel_id=1, replica_groups=mesh['rows'=64,'cols'=4] {'rows'}, use_global_device_ids=true, to_apply=%region_14.0 | all-reduce | flops 128 | bytes 1024 | tf_op jit(solution)/shard_map/psum | solution.py:80
  767.9 0.9 multiply_add_fusion
  (14 shorter events, 0.1 us)
Async XLA Ops:
  0.0 8.7 %copy-start = (f32[1024,128]{1,0:T(8,128)S(1)}, f32[1024,128]{1,0:T(8,128)}, u32[]{:S(2)}) copy-start(f32[1024,128]{1,0:T(8,128)} %param.5) | copy-start | bytes 1572868
  0.0 14.3 %copy-start.1 = (s32[4,12]{1,0:T(4,128)S(1)}, s32[4,12]{1,0:T(4,128)}, u32[]{:S(2)}) copy-start(s32[4,12]{1,0:T(4,128)} %param.4) | copy-start | bytes 580
  3.1 42.6 %collective-permute-start.1 = (bf16[4,256,512]{2,1,0:T(8,128)(2,1)S(1)}, bf16[4,256,512]{2,1,0:T(8,128)(2,1)S(1)}, u32[]{:S(2)}, u32[]{:S(2)}) collective-permute-start(bf16[4,256,512]{2,1,0:T(8,128)(2,1)S(1)} %bitcast.26), channel_id=1, source_target_pairs={{4,0},{8,4},{12,8},{16,12},{20,16},{24,20},{28,24},{32,28},{36,32}... | collective-permute-start | bytes 3145736 | tf_op jit(solution)/shard_map/ppermute | solution.py:21
  5.7 40.0 %collective-permute-start = (bf16[4,256,512]{2,1,0:T(8,128)(2,1)S(1)}, bf16[4,256,512]{2,1,0:T(8,128)(2,1)}, u32[]{:S(2)}, u32[]{:S(2)}) collective-permute-start(bf16[4,256,512]{2,1,0:T(8,128)(2,1)S(1)} %bitcast.27), channel_id=1, source_target_pairs={{0,4},{4,8},{8,12},{12,16},{16,20},{20,24},{24,28},{28,32},{32,36}... | collective-permute-start | bytes 3145736 | tf_op jit(solution)/shard_map/ppermute | solution.py:20
  8.7 55.9 %collective-permute-start.5 = (f32[4,256,128]{2,1,0:T(8,128)S(1)}, f32[4,256,128]{2,1,0:T(8,128)S(1)}, u32[]{:S(2)}, u32[]{:S(2)}) collective-permute-start(f32[4,256,128]{2,1,0:T(8,128)S(1)} %bitcast.20), channel_id=1, source_target_pairs={{4,0},{8,4},{12,8},{16,12},{20,16},{24,20},{28,24},{32,28},{36,32}... | collective-permute-start | bytes 1572872 | tf_op jit(solution)/shard_map/ppermute | solution.py:21
  11.3 53.4 %collective-permute-start.4 = (f32[4,256,128]{2,1,0:T(8,128)S(1)}, f32[4,256,128]{2,1,0:T(8,128)}, u32[]{:S(2)}, u32[]{:S(2)}) collective-permute-start(f32[4,256,128]{2,1,0:T(8,128)S(1)} %bitcast.21), channel_id=1, source_target_pairs={{0,4},{4,8},{8,12},{12,16},{16,20},{20,24},{24,28},{28,32},{32,36}... | collective-permute-start | bytes 1572872 | tf_op jit(solution)/shard_map/ppermute | solution.py:20
  56.6 9.2 %collective-permute-start.3 = (f32[4,256]{1,0:T(4,128)S(1)}, f32[4,256]{1,0:T(4,128)S(1)}, u32[]{:S(2)}, u32[]{:S(2)}) collective-permute-start(f32[4,256]{1,0:T(4,128)S(1)} %rsqrt.21), channel_id=1, source_target_pairs={{4,0},{8,4},{12,8},{16,12},{20,16},{24,20},{28,24},{32,28},{36,32}... | collective-permute-start | bytes 12296 | tf_op jit(solution)/shard_map/ppermute | solution.py:21
  62.5 7.6 collective-permute-start.2
  336.9 10.8 %collective-permute-start.7 = (f32[4,256,128]{2,1,0:T(8,128)S(1)}, f32[4,256,128]{2,1,0:T(8,128)S(1)}, u32[]{:S(2)}, u32[]{:S(2)}) collective-permute-start(f32[4,256,128]{2,1,0:T(8,128)S(1)} %bitcast.23), channel_id=1, source_target_pairs={{4,0},{8,4},{12,8},{16,12},{20,16},{24,20},{28,24},{32,28},{36,32}... | collective-permute-start | bytes 1572872 | tf_op jit(solution)/shard_map/ppermute | solution.py:21
  339.5 9.1 %collective-permute-start.6 = (f32[4,256,128]{2,1,0:T(8,128)S(1)}, f32[4,256,128]{2,1,0:T(8,128)S(1)}, u32[]{:S(2)}, u32[]{:S(2)}) collective-permute-start(f32[4,256,128]{2,1,0:T(8,128)S(1)} %bitcast.24), channel_id=1, source_target_pairs={{0,4},{4,8},{8,12},{12,16},{16,20},{20,24},{24,28},{28,32},{32,36}... | collective-permute-start | bytes 1572872 | tf_op jit(solution)/shard_map/ppermute | solution.py:20
  614.7 10.8 %collective-permute-start.9 = (f32[4,256,128]{2,1,0:T(8,128)S(1)}, f32[4,256,128]{2,1,0:T(8,128)S(1)}, u32[]{:S(2)}, u32[]{:S(2)}) collective-permute-start(f32[4,256,128]{2,1,0:T(8,128)S(1)} %bitcast.30), channel_id=1, source_target_pairs={{4,0},{8,4},{12,8},{16,12},{20,16},{24,20},{28,24},{32,28},{36,32}... | collective-permute-start | bytes 1572872 | tf_op jit(solution)/shard_map/ppermute | solution.py:21
  617.3 9.1 %collective-permute-start.8 = (f32[4,256,128]{2,1,0:T(8,128)S(1)}, f32[4,256,128]{2,1,0:T(8,128)S(1)}, u32[]{:S(2)}, u32[]{:S(2)}) collective-permute-start(f32[4,256,128]{2,1,0:T(8,128)S(1)} %bitcast.31), channel_id=1, source_target_pairs={{0,4},{4,8},{8,12},{12,16},{16,20},{20,24},{24,28},{28,32},{32,36}... | collective-permute-start | bytes 1572872 | tf_op jit(solution)/shard_map/ppermute | solution.py:20
where the time goes:
time: 770 us; the launch traced here: 769 us
  blocking collectives  634 us (82%)
  matrix products  49.4 us (6%)
  local copies, waits for them, and re-layouts  31.3 us (4%)
  starting transfers between devices  30.3 us (4%)
  waiting for transfers between devices  16.5 us (2%)
    psum x3, blocking collectives, squares(): return lax.psum(column_sums(residual, residual), 'rows')  377 us
    psum x2, blocking collectives, shards(): curvature = lax.psum(column_sums(direction, image), 'rows')  256 us
    dot_general x3, matrix products, shards(): jnp.dot(banded, nearby.reshape(3 * own_rows, columns), precision=highest,...  39.9 us
    mul x2, local copies, waits for them, and re-layouts, shards(): cubed.reshape(own_blocks, block_rows, 3 * own_blocks, block_rows)  18.8 us
    ppermute x5, starting transfers between devices, extended(): after = lax.ppermute(leading, axis, down)  16.1 us
  transfers between devices with their start and end apart: 10, of which 5 were waited for; matrix products, arithmetic and copies ran while one was open for 6% of the time, Pallas kernels for 0%

commit v1 on v0

--- a/solution.py
+++ b/solution.py
@@ -77,7 +77,7 @@
             preferred_element_type=jnp.float32,
         )
         image = direction - diffusion * mixed
-        curvature = lax.psum(column_sums(direction, image), "rows")
+        curvature = jnp.sum(lax.all_gather(column_sums(direction, image), "rows"), axis=0)
         step_size = residual_sq / curvature
         solution = solution + step_size * direction
         residual = residual - step_size * image

time: 770 us -> 638 us (0.83)
  blocking collectives: 634 us -> 494 us
    psum x2 -> x0, blocking collectives: 256 us -> none  [shards(): curvature = lax.psum(column_sums(direction, image), 'rows')]
    all_gather x0 -> x3, blocking collectives: none -> 118 us  [shards(): lax.all_gather(column_sums(direction, image), 'rows')]
  transfers between devices with their start and end apart: 10 -> 10, of which waited for: 5 -> 5; matrix products, arithmetic and copies ran while one was open for 6% -> 7% of each run, Pallas kernels for 0% -> 0%
where the time goes in v1:
time: 638 us; the launch traced here: 632 us
  blocking collectives  494 us (77%)
  matrix products  49.4 us (8%)
  starting transfers between devices  33.3 us (5%)
  local copies, waits for them, and re-layouts  31.3 us (5%)
  waiting for transfers between devices  16.1 us (3%)
  other arithmetic  7.59 us (1%)
    psum x3, blocking collectives, squares(): return lax.psum(column_sums(residual, residual), 'rows')  376 us
    all_gather x3, blocking collectives, shards(): lax.all_gather(column_sums(direction, image), 'rows')  118 us
    dot_general x3, matrix products, shards(): jnp.dot(banded, nearby.reshape(3 * own_rows, columns), precision=highest,...  39.9 us
    ppermute x5, starting transfers between devices, extended(): after = lax.ppermute(leading, axis, down)  20.8 us
    mul x2, local copies, waits for them, and re-layouts, shards(): cubed.reshape(own_blocks, block_rows, 3 * own_blocks, block_rows)  18.8 us
  transfers between devices with their start and end apart: 10, of which 5 were waited for; matrix products, arithmetic and copies ran while one was open for 7% of the time, Pallas kernels for 0%

profile of v1, /device:TPU:145, one launch (start us, length us, event | category | flops | bytes accessed | tf_op | source)
XLA Modules:
  0.0 632.1 jit_solution(8565947439064509636)
XLA Ops:
  0.0 1.6 fusion.10
  1.6 1.5 fusion.11
  3.1 2.6 collective-permute-start.1
  5.7 3.0 collective-permute-start
  8.7 2.6 collective-permute-start.5
  11.3 3.0 collective-permute-start.4
  14.3 0.1 copy.6
  14.4 0.1 compare_reduce_fusion
  14.5 0.1 copy.7
  14.6 6.2 mul.127
  20.8 12.3 %copy.9 = f32[384,8,4,256]{3,1,2,0:T(8,128)} copy(f32[384,8,4,256]{3,2,1,0:T(4,128)} %bitcast.21) | data formatting | bytes 25165824
  33.1 12.6 %copy.8 = f32[1024,3072]{1,0:T(8,128)} copy(f32[1024,3072]{0,1:T(8,128)} %bitcast.22) | data formatting | bytes 25165824 | tf_op jit(solution)/shard_map/mul | solution.py:58
  45.7 0.0 collective-permute-done.1
  45.7 0.0 collective-permute-done
  45.7 1.4 pad_maximum_fusion
  47.1 9.5 %fusion.20 = (f32[1024]{0:T(1024)S(1)}, f32[1024,3072]{1,0:T(8,128)}) fusion(f32[1024,3072]{1,0:T(8,128)} %copy.8, bf16[1024,512]{1,0:T(8,128)(2,1)S(1)} %fusion.11, bf16[3072,512]{1,0:T(8,128)(2,1)S(1)} %bitcast.32), kind=kOutput, calls=%fused_computation.42 | convolution fusion | flops 3236953088 | bytes 29364224 | tf_op jit(solution)/shard_map/dot_general | solution.py:45
  56.6 5.9 collective-permute-start.3
  62.5 2.1 collective-permute-start.2
  64.6 0.0 collective-permute-done.4
  64.6 1.1 pad_maximum_fusion.1
  65.8 4.3 collective-permute-done.2
  70.2 13.3 %multiply_reduce_fusion.3 = (f32[128]{0:T(128)S(1)}, f32[128]{0:T(128)S(1)}, f32[1024,128]{1,0:T(8,128)S(1)}) fusion(f32[1024,128]{1,0:T(8,128)S(1)} %copy-done, f32[3072,128]{1,0:T(8,128)S(1)} %bitcast.36, f32[1024,3072]{1,0:T(8,128)} %get-tuple-element.10, f32[3072]{0:T(1024)S(1)} %mul.132, f32[1024]{0:T(1024)S(1)} %rsqrt.20), kind=kOutput, calls=%fused_computation.36 | convolution fusion | flops 4838916096 | bytes 15221760 | tf_op jit(solution)/shard_map/dot_general | solution.py:73
  83.5 129.1 %psum.21 = f32[128]{0:T(128)S(1)} all-reduce(f32[128]{0:T(128)S(1)} %get-tuple-element.6), channel_id=1, replica_groups=mesh['rows'=64,'cols'=4] {'rows'}, use_global_device_ids=true, to_apply=%region_1.0 | all-reduce | flops 128 | bytes 1024 | tf_op jit(solution)/shard_map/psum | solution.py:31
  212.6 36.0 %all-gather.3 = f32[64,1,128]{2,1,0:T(1,128)S(1)} all-gather(f32[1,1,128]{2,1,0:T(1,128)S(1)} %bitcast.39), channel_id=2, replica_groups=mesh['rows'=64,'cols'=4] {'rows'}, dimensions={0}, use_global_device_ids=true | all-gather | bytes 33280 | tf_op jit(solution)/shard_map/all_gather | solution.py:80
  248.5 0.1 reduce_sum.103
  248.6 0.2 multiply_reduce_fusion.2
  248.8 123.6 %psum.22 = f32[128]{0:T(128)S(1)} all-reduce(f32[128]{0:T(128)S(1)} %get-tuple-element.7), channel_id=1, replica_groups=mesh['rows'=64,'cols'=4] {'rows'}, use_global_device_ids=true, to_apply=%region_8.0 | all-reduce | flops 128 | bytes 1024 | tf_op jit(solution)/shard_map/psum | solution.py:31
  372.3 0.1 multiply_add_fusion.2
  372.4 4.9 collective-permute-start.7
  377.3 2.1 collective-permute-start.6
  379.5 3.4 collective-permute-done.7
  382.9 2.5 collective-permute-done.6
  385.4 0.1 pad_maximum_fusion.2
  385.5 13.3 %multiply_reduce_fusion.1 = (f32[128]{0:T(128)S(1)}, f32[1024,128]{1,0:T(8,128)S(1)}) fusion(f32[1024,128]{1,0:T(8,128)S(1)} %multiply_add_fusion.2, f32[3072,128]{1,0:T(8,128)S(1)} %bitcast.38, f32[1024,3072]{1,0:T(8,128)} %get-tuple-element.10, f32[3072]{0:T(1024)S(1)} %mul.132, f32[1024]{0:T(1024)S(1)} %rsqrt.20), kind=kOutput, calls=%fused_computation.32 | convolution fusion | flops 4838653952 | bytes 15221248 | tf_op jit(solution)/shard_map/dot_general | solution.py:73
  398.8 41.0 %all-gather.4 = f32[64,1,128]{2,1,0:T(1,128)S(1)} all-gather(f32[1,1,128]{2,1,0:T(1,128)S(1)} %bitcast.41), channel_id=3, replica_groups=mesh['rows'=64,'cols'=4] {'rows'}, dimensions={0}, use_global_device_ids=true | all-gather | bytes 33280 | tf_op jit(solution)/shard_map/all_gather | solution.py:80
  439.9 0.1 reduce_sum.106
  439.9 0.2 multiply_reduce_fusion
  440.1 123.6 %psum.23 = f32[128]{0:T(128)S(1)} all-reduce(f32[128]{0:T(128)S(1)} %multiply_reduce_fusion), channel_id=1, replica_groups=mesh['rows'=64,'cols'=4] {'rows'}, use_global_device_ids=true, to_apply=%region_12.0 | all-reduce | flops 128 | bytes 1024 | tf_op jit(solution)/shard_map/psum | solution.py:31
  563.7 0.1 multiply_add_fusion.1
  563.8 4.9 collective-permute-start.9
  568.7 2.2 collective-permute-start.8
  570.9 3.4 collective-permute-done.9
  574.3 2.5 collective-permute-done.8
  576.7 0.1 pad_maximum_fusion.3
  576.8 13.2 %fusion.19 = f32[128]{0:T(128)S(1)} fusion(f32[1024,128]{1,0:T(8,128)S(1)} %multiply_add_fusion.1, f32[3072,128]{1,0:T(8,128)S(1)} %bitcast.37, f32[1024,3072]{1,0:T(8,128)} %get-tuple-element.10, f32[3072]{0:T(1024)S(1)} %mul.132, f32[1024]{0:T(1024)S(1)} %rsqrt.20), kind=kOutput, calls=%fused_computation.27 | convolution fusion | flops 4838653952 | bytes 14696960 | tf_op jit(solution)/shard_map/dot_general | solution.py:73
  590.1 41.0 %all-gather.5 = f32[64,1,128]{2,1,0:T(1,128)S(1)} all-gather(f32[1,1,128]{2,1,0:T(1,128)S(1)} %bitcast.40), channel_id=4, replica_groups=mesh['rows'=64,'cols'=4] {'rows'}, dimensions={0}, use_global_device_ids=true | all-gather | bytes 33280 | tf_op jit(solution)/shard_map/all_gather | solution.py:80
  631.1 0.1 reduce_sum.109
  631.2 0.9 multiply_add_fusion
  (18 shorter events, 0.1 us)
Async XLA Ops:
  0.0 8.7 %copy-start = (f32[1024,128]{1,0:T(8,128)S(1)}, f32[1024,128]{1,0:T(8,128)}, u32[]{:S(2)}) copy-start(f32[1024,128]{1,0:T(8,128)} %param.5) | copy-start | bytes 1572868
  0.0 14.3 %copy-start.1 = (s32[4,12]{1,0:T(4,128)S(1)}, s32[4,12]{1,0:T(4,128)}, u32[]{:S(2)}) copy-start(s32[4,12]{1,0:T(4,128)} %param.4) | copy-start | bytes 580
  3.1 42.6 %collective-permute-start.1 = (bf16[4,256,512]{2,1,0:T(8,128)(2,1)S(1)}, bf16[4,256,512]{2,1,0:T(8,128)(2,1)S(1)}, u32[]{:S(2)}, u32[]{:S(2)}) collective-permute-start(bf16[4,256,512]{2,1,0:T(8,128)(2,1)S(1)} %bitcast.29), channel_id=1, source_target_pairs={{4,0},{8,4},{12,8},{16,12},{20,16},{24,20},{28,24},{32,28},{36,32}... | collective-permute-start | bytes 3145736 | tf_op jit(solution)/shard_map/ppermute | solution.py:21
  5.7 40.0 %collective-permute-start = (bf16[4,256,512]{2,1,0:T(8,128)(2,1)S(1)}, bf16[4,256,512]{2,1,0:T(8,128)(2,1)}, u32[]{:S(2)}, u32[]{:S(2)}) collective-permute-start(bf16[4,256,512]{2,1,0:T(8,128)(2,1)S(1)} %bitcast.30), channel_id=1, source_target_pairs={{0,4},{4,8},{8,12},{12,16},{16,20},{20,24},{24,28},{28,32},{32,36}... | collective-permute-start | bytes 3145736 | tf_op jit(solution)/shard_map/ppermute | solution.py:20
  8.7 55.9 %collective-permute-start.5 = (f32[4,256,128]{2,1,0:T(8,128)S(1)}, f32[4,256,128]{2,1,0:T(8,128)S(1)}, u32[]{:S(2)}, u32[]{:S(2)}) collective-permute-start(f32[4,256,128]{2,1,0:T(8,128)S(1)} %bitcast.23), channel_id=1, source_target_pairs={{4,0},{8,4},{12,8},{16,12},{20,16},{24,20},{28,24},{32,28},{36,32}... | collective-permute-start | bytes 1572872 | tf_op jit(solution)/shard_map/ppermute | solution.py:21
  11.3 53.4 %collective-permute-start.4 = (f32[4,256,128]{2,1,0:T(8,128)S(1)}, f32[4,256,128]{2,1,0:T(8,128)}, u32[]{:S(2)}, u32[]{:S(2)}) collective-permute-start(f32[4,256,128]{2,1,0:T(8,128)S(1)} %bitcast.24), channel_id=1, source_target_pairs={{0,4},{4,8},{8,12},{12,16},{16,20},{20,24},{24,28},{28,32},{32,36}... | collective-permute-start | bytes 1572872 | tf_op jit(solution)/shard_map/ppermute | solution.py:20
  56.6 9.2 %collective-permute-start.3 = (f32[4,256]{1,0:T(4,128)S(1)}, f32[4,256]{1,0:T(4,128)S(1)}, u32[]{:S(2)}, u32[]{:S(2)}) collective-permute-start(f32[4,256]{1,0:T(4,128)S(1)} %rsqrt.21), channel_id=1, source_target_pairs={{4,0},{8,4},{12,8},{16,12},{20,16},{24,20},{28,24},{32,28},{36,32}... | collective-permute-start | bytes 12296 | tf_op jit(solution)/shard_map/ppermute | solution.py:21
  62.5 7.6 %collective-permute-start.2 = (f32[4,256]{1,0:T(4,128)S(1)}, f32[4,256]{1,0:T(4,128)S(1)}, u32[]{:S(2)}, u32[]{:S(2)}) collective-permute-start(f32[4,256]{1,0:T(4,128)S(1)} %rsqrt.21), channel_id=1, source_target_pairs={{0,4},{4,8},{8,12},{12,16},{16,20},{20,24},{24,28},{28,32},{32,36}... | collective-permute-start | bytes 12296 | tf_op jit(solution)/shard_map/ppermute | solution.py:20
  372.4 10.5 %collective-permute-start.7 = (f32[4,256,128]{2,1,0:T(8,128)S(1)}, f32[4,256,128]{2,1,0:T(8,128)S(1)}, u32[]{:S(2)}, u32[]{:S(2)}) collective-permute-start(f32[4,256,128]{2,1,0:T(8,128)S(1)} %bitcast.26), channel_id=1, source_target_pairs={{4,0},{8,4},{12,8},{16,12},{20,16},{24,20},{28,24},{32,28},{36,32}... | collective-permute-start | bytes 1572872 | tf_op jit(solution)/shard_map/ppermute | solution.py:21
  377.3 8.0 %collective-permute-start.6 = (f32[4,256,128]{2,1,0:T(8,128)S(1)}, f32[4,256,128]{2,1,0:T(8,128)S(1)}, u32[]{:S(2)}, u32[]{:S(2)}) collective-permute-start(f32[4,256,128]{2,1,0:T(8,128)S(1)} %bitcast.27), channel_id=1, source_target_pairs={{0,4},{4,8},{8,12},{12,16},{16,20},{20,24},{24,28},{28,32},{32,36}... | collective-permute-start | bytes 1572872 | tf_op jit(solution)/shard_map/ppermute | solution.py:20
  563.8 10.5 %collective-permute-start.9 = (f32[4,256,128]{2,1,0:T(8,128)S(1)}, f32[4,256,128]{2,1,0:T(8,128)S(1)}, u32[]{:S(2)}, u32[]{:S(2)}) collective-permute-start(f32[4,256,128]{2,1,0:T(8,128)S(1)} %bitcast.33), channel_id=1, source_target_pairs={{4,0},{8,4},{12,8},{16,12},{20,16},{24,20},{28,24},{32,28},{36,32}... | collective-permute-start | bytes 1572872 | tf_op jit(solution)/shard_map/ppermute | solution.py:21
  568.7 8.0 %collective-permute-start.8 = (f32[4,256,128]{2,1,0:T(8,128)S(1)}, f32[4,256,128]{2,1,0:T(8,128)S(1)}, u32[]{:S(2)}, u32[]{:S(2)}) collective-permute-start(f32[4,256,128]{2,1,0:T(8,128)S(1)} %bitcast.34), channel_id=1, source_target_pairs={{0,4},{4,8},{8,12},{12,16},{16,20},{20,24},{24,28},{28,32},{32,36}... | collective-permute-start | bytes 1572872 | tf_op jit(solution)/shard_map/ppermute | solution.py:20
